TPU v7x, 32 devices: a whole 2x2x4 slice. The times are simulated.
32 devices in a mesh: bx: 4 (over y, x), by: 8 (over z, core).
Axes of the slice: x: 2, y: 2, z: 4, core: 2. Of those that a mesh axis runs over, the one named last changes fastest.
Arguments:
- terminal_value: float32 [64, 128, 256], P('bx', 'by'), may hold values from -3 to 3
- density: float32 [64, 128, 256], P('bx', 'by')
- potential: float32 [64, 128, 256], P('bx', 'by'), may hold values from -5 to 5
- heights: int32 [64, 128], P('bx', 'by'), may hold values from 0 to 64
Outputs:
- value_field: float32 [64, 128, 256], P('bx', 'by')
- density_next: float32 [64, 128, 256], P('bx', 'by')
All inputs are finite; a program needn't handle non-finite values.
Results may differ from a plain program's by a relative error of at most 0.0001.
Values sent between devices are 32-bit elements; how exact they have to be, the bound alone decides.
A program may use at most 64 MiB of HBM per device.

v0:
```python
import functools

import jax
import jax.numpy as jnp
from jax import lax
from jax.experimental import pallas as pl
from jax.experimental.pallas import tpu as pltpu
from jax.sharding import PartitionSpec as P

DT_HJB = 0.5
NU_HJB = 0.25
COUPLE = 0.5
PENALTY = 2.0
DT_FP = 0.25
ABSORB = 4.0
SHIFT = 7.0

X0 = 4
HALO = 8
MESH = pl.DeviceIdType.MESH


class Link:
    def __init__(self, src, dst, send, recv, device, can_send, can_recv):
        self.copy = pltpu.make_async_remote_copy(
            src_ref=src, dst_ref=dst, send_sem=send, recv_sem=recv,
            device_id=device, device_id_type=MESH)
        self.can_send, self.can_recv = can_send, can_recv

    def start(self):
        pl.when(self.can_send)(lambda: self.copy.start())

    def wait_recv(self):
        pl.when(self.can_recv)(lambda: self.copy.wait_recv())

    def wait_send(self):
        pl.when(self.can_send)(lambda: self.copy.wait_send())


def kernel(nbx, nby, t_in, m_in, p_in, h_in, v_out, s_out,
           T, C, D, M, V, G, B1, Q, D4, POT, HB, PKS, PKR, GR, PA, PB,
           ssem, rsem, asend, arecv, bsend, brecv, lsem):
    nx, ny, nz = POT.shape
    bx, by = lax.axis_index("bx"), lax.axis_index("by")
    XE, YE, X1 = nx + 2 * X0, ny + HALO, X0 + nx
    barrier = pltpu.get_barrier_semaphore()
    for k in range(1, nby):
        pl.semaphore_signal(barrier, inc=1, device_id=(bx, lax.rem(by + k, nby)), device_id_type=MESH)
    for k in range(1, nbx):
        pl.semaphore_signal(barrier, inc=1, device_id=(lax.rem(bx + k, nbx), by), device_id_type=MESH)

    rows = pl.ds(0, ny)
    beyond = pl.ds(ny, HALO)
    loads = [
        pltpu.make_async_copy(h_in, HB.at[1, 1], lsem.at[3]),
        pltpu.make_async_copy(m_in, D.at[pl.ds(X0, nx), rows], lsem.at[1]),
        pltpu.make_async_copy(p_in, POT, lsem.at[2]),
        pltpu.make_async_copy(t_in, T.at[pl.ds(X0, nx), rows], lsem.at[0]),
    ]
    for c in loads:
        c.start()

    has_xl, has_xu = bx > 0, bx < nbx - 1
    has_yl, has_yu = by > 0, by < nby - 1
    count = [0]

    def link(src, dst, device, can_send, can_recv):
        i = count[0]
        count[0] += 1
        return Link(src, dst, ssem.at[i], rsem.at[i], device, can_send, can_recv)

    def x_up(src, dst):
        return link(src, dst, (bx + 1, by), has_xu, has_xl)

    def x_down(src, dst):
        return link(src, dst, (bx - 1, by), has_xl, has_xu)

    def y_up(src, dst, has=True):
        return link(src, dst, (bx, by + 1), has_yu & has, has_yl & has)

    def y_down(src, dst, has=True):
        return link(src, dst, (bx, by - 1), has_yl & has, has_yu & has)

    def x_links(buf, w):
        return [x_up(buf.at[pl.ds(X1 - w, w), rows], buf.at[pl.ds(X0 - w, w), rows]),
                x_down(buf.at[pl.ds(X0, w), rows], buf.at[pl.ds(X1, w), rows])]

    def packed_links(planes):
        return [y_up(PKS.at[0, planes], PKR.at[0, planes]), y_down(PKS.at[1, planes], PKR.at[1, planes])]

    def field_links(planes):
        return [y_up(G.at[planes, pl.ds(ny - 8, 8)], GR.at[0, planes]),
                y_down(G.at[planes, pl.ds(0, 8)], GR.at[1, planes])]

    def zero_planes(lo):
        for buf in (T, C, D, G):
            buf[pl.ds(lo, X0)] = jnp.zeros((X0, YE, nz), jnp.float32)

    pl.when(jnp.logical_not(has_xl))(lambda: zero_planes(0))
    pl.when(jnp.logical_not(has_xu))(lambda: zero_planes(X1))

    def column(side, part, x, n, first):
        line = HB[side, part, pl.ds(x, 1), :].astype(jnp.float32)
        lanes = lax.broadcasted_iota(jnp.int32, (n, ny), 1)
        subs = lax.broadcasted_iota(jnp.int32, (n, ny), 0) + first
        return jnp.sum(jnp.where(lanes == subs, line, 0.0), axis=1, keepdims=True)

    def level_mask(col, high):
        level = lax.broadcasted_iota(jnp.int32, (col.shape[0], nz), 1).astype(jnp.float32)
        return jnp.where(level < col, high, 0.0)

    for c in loads[:3]:
        c.wait()

    @pl.loop(0, nx)
    def _(x):
        b = level_mask(column(1, 1, x, ny, 0), ABSORB)
        D4[X0 + x, rows, :] = b
        C[X0 + x, rows, :] = POT[x] + COUPLE * D[X0 + x, rows, :] + (PENALTY / ABSORB) * b

    loads[3].wait()
    row8 = lax.broadcasted_iota(jnp.int32, (8, nz), 0)

    def pack(i, with_density):
        ys = pl.ds(ny - 8, 8)
        low = pltpu.roll(D[i, ys, :], 3, 0) if with_density else jnp.zeros((8, nz), jnp.float32)
        PKS[0, i] = jnp.where(row8 >= 5, T[i, ys, :], jnp.where(row8 >= 3, pltpu.roll(C[i, ys, :], 5, 0), low))
        ys = pl.ds(0, 8)
        high = pltpu.roll(D[i, ys, :], 5, 0) if with_density else jnp.zeros((8, nz), jnp.float32)
        PKS[1, i] = jnp.where(row8 < 3, T[i, ys, :], jnp.where(row8 < 5, pltpu.roll(C[i, ys, :], 3, 0), high))

    @pl.loop(X0, X1)
    def _(i):
        pack(i, True)

    pl.semaphore_wait(barrier, (nby - 1) + (nbx - 1))

    hx = [x_up(HB.at[1, 1], HB.at[0, 1]), x_down(HB.at[1, 1], HB.at[2, 1])]
    hy = [y_up(HB.at[1, 1], HB.at[1, 0]), y_down(HB.at[1, 1], HB.at[1, 2])]
    half = nx // 2
    py, pz = packed_links(pl.ds(X0, half)), packed_links(pl.ds(X0 + half, nx - half))
    tx, cx, dx = x_links(T, 3), x_links(C, 2), x_links(D, 1)
    for c in hx + hy + py + tx + pz + cx + dx:
        c.start()

    keep = (row8 >= jnp.where(has_yu, 0, 4)) & (row8 < jnp.where(has_yl, 8, 4))
    upper = row8 < 4

    def join(a, b):
        return jnp.where(keep, jnp.where(upper, b, a), 0.0)

    def unpack(i):
        a, b = PKR[0, i], PKR[1, i]
        T[i, beyond, :] = join(a, b)
        C[i, beyond, :] = join(pltpu.roll(a, 3, 0), pltpu.roll(b, 5, 0))
        D[i, beyond, :] = join(pltpu.roll(a, 5, 0), pltpu.roll(b, 3, 0))

    def loop(lo, hi, f):
        step = 4 if (hi - lo) % 4 == 0 else 1

        @pl.loop(0, (hi - lo) // step)
        def _(j):
            for k in range(step):
                f(lo + step * j + k)

    def pairs(lo, hi, value, store):
        @pl.loop(0, (hi - lo) // 2)
        def _(j):
            i = lo + 2 * j
            a, b = value(i), value(i + 1)
            store(i, a)
            store(i + 1, b)

    def ends(k, e, value, store):
        @pl.loop(0, k + e)
        def _(j):
            i, n = X0 - k + j, X1 - e + j
            a, b = value(i), value(n)
            store(i, a)
            store(n, b)

    def clear(buf, k):
        def zero(lo):
            buf[pl.ds(lo, k)] = jnp.zeros((k, YE, nz), jnp.float32)
        pl.when(jnp.logical_not(has_xl))(lambda: zero(X0 - k))
        pl.when(jnp.logical_not(has_xu))(lambda: zero(X1))

    lane = lax.broadcasted_iota(jnp.int32, (YE, 128), 1)

    def z_up(v):
        n = v.shape[0]
        tiles = [pltpu.roll(v[:, j:j + 128], 127, 1) for j in range(0, nz, 128)]
        tiles.append(jnp.zeros_like(tiles[0]))
        return jnp.concatenate([jnp.where(lane[:n] == 127, b, a) for a, b in zip(tiles, tiles[1:])], axis=1)

    def z_low(v, edge=None):
        n = v.shape[0]
        tiles = [jnp.zeros((n, 128), jnp.float32) if edge is None else edge]
        tiles += [pltpu.roll(v[:, j:j + 128], 1, 1) for j in range(0, nz, 128)]
        return jnp.concatenate([jnp.where(lane[:n] == 0, a, b) for a, b in zip(tiles, tiles[1:])], axis=1)

    def put(dst, i, v):
        dst[i, rows, :] = v[:ny]
        dst[i, beyond, :] = jnp.where(keep, v[ny:], 0.0)

    def hjb(src):
        def f(i):
            v = src[i]
            lap = -6.0 * v
            ham = jnp.zeros_like(v)
            for u, l in ((src[i + 1], src[i - 1]), (pltpu.roll(v, YE - 1, 0), pltpu.roll(v, 1, 0)),
                         (z_up(v), z_low(v))):
                lap = lap + (u + l)
                ham = ham + jnp.square(jnp.maximum(v - l, 0.0)) + jnp.square(jnp.minimum(u - v, 0.0))
            return v + DT_HJB * (NU_HJB * lap - 0.5 * ham + C[i])
        return f

    def put_mid(i, v):
        put(M, i, v)

    def put_halo(i, v):
        put(V, i, v)

    def put_value(i, v):
        put(V, i, v)
        v_out[i - X0] = v[:ny]

    def flux(v, vu, m, mu):
        s = v - vu
        return jnp.maximum(s, 0.0) * m + jnp.minimum(s, 0.0) * mu

    def x_flux(i):
        return flux(V[i, rows, :], V[i + 1, rows, :], D[i, rows, :], D[i + 1, rows, :])

    def transport(starts, n):
        def one(i, before):
            v, m = V[i], D[i]
            fy = flux(v, pltpu.roll(v, YE - 1, 0), m, pltpu.roll(m, YE - 1, 0))
            ly = pltpu.roll(fy, 1, 0)[:ny]
            v, m = v[:ny], m[:ny]
            fz = flux(v, z_up(v), m, z_up(m))
            lz = z_low(fz, jnp.minimum(-v[:, :128], 0.0) * m[:, :128])
            fx = x_flux(i)
            return fx, m - DT_FP * ((fx - before) + (fy[:ny] - ly) + (fz - lz))

        def f(j, before):
            done = [one(lo + j, b) for lo, b in zip(starts, before)]
            for lo, d in zip(starts, done):
                G[lo + j, rows, :] = d[1]
            return tuple(d[0] for d in done)
        lax.fori_loop(0, n, f, tuple(x_flux(lo - 1) for lo in starts))

    def beyond_obstacles(side, x, i):
        col = jnp.where(lax.broadcasted_iota(jnp.int32, (8, 1), 0) < 4,
                        column(side, 2, x, 8, 0), column(side, 0, x, 8, ny - 8))
        D4[i, beyond, :] = level_mask(col, ABSORB)

    for c in hy + py:
        c.wait_recv()
    loop(X0, X0 + half, unpack)
    pairs(X0 + 1, X0 + half - 1, hjb(T), put_mid)
    for c in pz:
        c.wait_recv()
    loop(X0 + half, X1, unpack)
    pairs(X0 + half - 1, X1 - 1, hjb(T), put_mid)
    pairs(X0 + 2, X1 - 2, hjb(M), put_value)
    for c in hx + tx + cx:
        c.wait_recv()
    corners = ((0, has_xl, X0 - 2), (2, has_xu, X1))
    pc = []
    for side, has, lo in corners:
        loop(lo, lo + 2, lambda i: pack(i, False))
        pc += packed_links(pl.ds(lo, 2))
        pc.append(y_up(HB.at[side, 1], HB.at[side, 0], has))
        pc.append(y_down(HB.at[side, 1], HB.at[side, 2], has))
    for c in pc:
        c.start()
    transport((X0 + 3, X0 + half), half - 3)
    gi = field_links(pl.ds(X0 + 3, nx - 6))
    for c in gi:
        c.start()
    loop(0, nx, lambda x: beyond_obstacles(1, x, X0 + x))

    for c in dx + pc:
        c.wait_recv()
    for side, has, lo in corners:
        loop(lo, lo + 2, unpack)
    ends(2, 1, hjb(T), put_mid)
    clear(M, 2)
    ends(0, 2, hjb(M), put_value)
    for i in (X0 - 1, X1):
        put_halo(i, hjb(M)(i))
    clear(V, 1)
    transport((X0, X1 - 3), 3)

    gx = x_links(G, 4)
    gy = field_links(pl.ds(X0, 3)) + field_links(pl.ds(X1 - 3, 3))
    for c in gx + gy:
        c.start()

    def halo_obstacles(side, x, i):
        D4[i, rows, :] = level_mask(column(side, 1, x, ny, 0), ABSORB)
        beyond_obstacles(side, x, i)

    @pl.loop(0, 3)
    def _(j):
        halo_obstacles(0, nx - 3 + j, X0 - 3 + j)
        halo_obstacles(2, j, X1 + j)

    def merge(i):
        G[i, beyond, :] = join(GR[0, i], GR[1, i])

    def shifted(src):
        def f(i):
            v = src[i]
            return D4[i] * v - ((src[i + 1] + src[i - 1]) + (pltpu.roll(v, YE - 1, 0) + pltpu.roll(v, 1, 0))
                                + (z_up(v) + z_low(v)))
        return f

    R = M

    def residual(i):
        return (1.0 - SHIFT) * G[i] - shifted(G)(i)

    def into(dst):
        return lambda i, v: put(dst, i, v)

    def moments(i, sums):
        r, b = R[i, rows, :], B1[i, rows, :]
        full = Q[i]
        yu = pltpu.roll(full, YE - 1, 0)[:ny]
        q = full[:ny]
        image = D4[i, rows, :] * q - 2.0 * (Q[i + 1, rows, :] + yu + z_up(q))
        terms = (r * r, r * b, b * b, b * q, q * q, q * image)

        def fold(a):
            a = a.reshape(ny // 8, 8, nz).sum(axis=0)
            return sum(a[:, j:j + 128] for j in range(0, nz, 128))

        return tuple(s + fold(a) for s, a in zip(sums, terms))

    for c in gi + gy:
        c.wait_recv()
    loop(X0, X1, merge)
    pairs(X0 + 1, X1 - 1, residual, into(R))
    pairs(X0 + 2, X1 - 2, shifted(R), into(B1))
    for c in gx:
        c.wait_recv()
    gc = field_links(pl.ds(1, 3)) + field_links(pl.ds(X1, 3))
    for c in gc:
        c.start()
    pairs(X0 + 3, X1 - 3, shifted(B1), into(Q))

    def two(j, sums):
        return moments(X0 + 4 + 2 * j, moments(X0 + 3 + 2 * j, sums))

    zero = jnp.zeros((8, 128), jnp.float32)
    sums = lax.fori_loop(0, (nx - 8) // 2, two, (zero,) * 6)

    for c in gc:
        c.wait_recv()
    loop(1, X0, merge)
    loop(X1, X1 + 3, merge)
    ends(3, 1, residual, into(R))
    clear(R, 3)
    ends(2, 2, shifted(R), into(B1))
    clear(B1, 2)
    ends(1, 3, shifted(B1), into(Q))
    clear(Q, 1)

    def rest(j, sums):
        for k in (2 * j, 2 * j + 1):
            sums = moments(X0 + k + jnp.where(k >= 3, nx - 8, 0), sums)
        return sums

    sums = lax.fori_loop(0, 4, rest, sums)
    tile_row = lax.broadcasted_iota(jnp.int32, (8, 128), 0)
    tile = zero
    for k, s in enumerate(sums):
        tile = jnp.where(tile_row == k, jnp.sum(s, axis=0, keepdims=True), tile)
    tile = jnp.sum(tile, axis=1, keepdims=True)
    tile = jnp.sum(jnp.where(tile_row == lane[:8], tile, 0.0), axis=0, keepdims=True)

    def all_sum(slots, value, n, me, device, send, recv):
        slots[me] = value
        copies = []
        for k in range(1, n):
            c = pltpu.make_async_remote_copy(
                src_ref=slots.at[me], dst_ref=slots.at[me], send_sem=send.at[k - 1], recv_sem=recv.at[k - 1],
                device_id=device(lax.rem(me + k, n)), device_id_type=MESH)
            c.start()
            copies.append(c)
        for k in range(1, n):
            source = lax.rem(me + n - k, n)
            pltpu.make_async_remote_copy(
                src_ref=slots.at[source], dst_ref=slots.at[source], send_sem=send.at[k - 1], recv_sem=recv.at[k - 1],
                device_id=device(source), device_id_type=MESH).wait_recv()
        return copies, jnp.sum(slots[...], axis=0)

    ca, tile = all_sum(PA, tile, nby, by, lambda j: (bx, j), asend, arecv)
    cb, tile = all_sum(PB, tile, nbx, bx, lambda j: (j, by), bsend, brecv)
    nu = [jnp.broadcast_to(tile[:, k:k + 1], (1, 128)) for k in range(6)]

    def dot(p, q, s):
        total = 0.0
        for i, a in enumerate(p):
            for j, b in enumerate(q):
                total = total + a * b * nu[i + j + s]
        return total

    def energy(p):
        return SHIFT * dot(p, p, 0) + dot(p, p, 1)

    def step_of(rr, p):
        return jnp.clip(rr / energy(p), 1.0 / 17.0, 1.0)

    one = jnp.ones_like(nu[0])
    rr = nu[0]
    p, r = (one,), (one,)
    x = None
    for it in range(3):
        a = step_of(rr, p)
        x = [a * c for c in p] if x is None else [x[j] + a * p[j] if j < len(x) else a * p[j] for j in range(len(p))]
        if it == 2:
            break
        image = [SHIFT * c for c in p] + [jnp.zeros_like(one)]
        for j, c in enumerate(p):
            image[j + 1] = image[j + 1] + c
        r = tuple((r[j] if j < len(r) else 0.0) - a * image[j] for j in range(len(image)))
        new = jnp.maximum(dot(r, r, 0), 0.0)
        beta = new / rr
        p = tuple(r[j] + (beta * p[j] if j < len(p) else 0.0) for j in range(len(r)))
        rr = new
    x = [jnp.concatenate([c] * (nz // 128), axis=1) for c in x]

    def finish(i):
        s_out[i - X0] = G[i, rows, :] + x[0] * R[i, rows, :] + x[1] * B1[i, rows, :] + x[2] * Q[i, rows, :]

    loop(X0, X1, finish)

    for c in hx + hy + tx + py + pz + cx + dx + pc + gx + gi + gy + gc:
        c.wait_send()
    for c in ca + cb:
        c.wait_send()


LINKS = 40


def per_device(nbx, nby, t, m, p, h):
    nx, ny, nz = t.shape
    ext = pltpu.VMEM((nx + 2 * X0, ny + HALO, nz), jnp.float32)
    packed = pltpu.VMEM((2, nx + 2 * X0, 8, nz), jnp.float32)
    out = jax.ShapeDtypeStruct(t.shape, jnp.float32)
    return pl.pallas_call(
        functools.partial(kernel, nbx, nby),
        out_shape=(out, out),
        in_specs=[pl.BlockSpec(memory_space=pl.ANY)] * 4,
        out_specs=(pl.BlockSpec(memory_space=pltpu.VMEM),) * 2,
        scratch_shapes=[ext] * 9 + [
            pltpu.VMEM((nx, ny, nz), jnp.float32), pltpu.VMEM((3, 3, nx, ny), jnp.int32), packed, packed, packed,
            pltpu.VMEM((nby, 1, 128), jnp.float32), pltpu.VMEM((nbx, 1, 128), jnp.float32),
            pltpu.SemaphoreType.DMA((LINKS,)), pltpu.SemaphoreType.DMA((LINKS,)),
            pltpu.SemaphoreType.DMA((nby - 1,)), pltpu.SemaphoreType.DMA((nby - 1,)),
            pltpu.SemaphoreType.DMA((nbx - 1,)), pltpu.SemaphoreType.DMA((nbx - 1,)),
            pltpu.SemaphoreType.DMA((4,)),
        ],
        compiler_params=pltpu.CompilerParams(collective_id=0, has_side_effects=True, vmem_limit_bytes=56_000_000),
        name="mean_field_step",
    )(t, m, p, h)


def solution(mesh):
    cells, plane = P("bx", "by", None), P("bx", "by")
    return jax.shard_map(
        functools.partial(per_device, mesh.shape["bx"], mesh.shape["by"]),
        mesh=mesh, in_specs=(cells, cells, cells, plane), out_specs=(cells, cells), check_vma=False)
```

profile of v0, /device:TPU:0, one launch (start us, length us, event | category | flops | bytes accessed | tf_op | source)
XLA Modules:
  0.0 34.1 jit_solution(4221636209662817235)
XLA Ops:
  0.6 0.0 copy-start
  0.6 0.7 %copy-done = s32[16,16]{1,0:T(8,128)S(1)} copy-done((s32[16,16]{1,0:T(8,128)S(1)}, s32[16,16]{1,0:T(8,128)}, u32[]{:S(2)}) %copy-start) | copy-done | bytes 1048
  1.3 31.4 %mean_field_step.1 = (f32[16,16,256]{2,1,0:T(8,128)S(1)}, f32[16,16,256]{2,1,0:T(8,128)S(1)}) custom-call(f32[16,16,256]{2,1,0:T(8,128)} %t_in.1, f32[16,16,256]{2,1,0:T(8,128)} %m_in.1, f32[16,16,256]{2,1,0:T(8,128)} %p_in.1, s32[16,16]{1,0:T(8,128)S(1)} %copy-done), custom_call_target="tpu_custom_call" | custom-call | tf_op jit(solution)/shard_map/mean_field_step/pallas_call | solution.py:455
  32.7 0.7 %copy.8 = f32[16,16,256]{2,1,0:T(8,128)} copy(f32[16,16,256]{2,1,0:T(8,128)S(1)} %get-tuple-element.4) | data formatting | bytes 524288
  33.4 0.7 %copy.9 = f32[16,16,256]{2,1,0:T(8,128)} copy(f32[16,16,256]{2,1,0:T(8,128)S(1)} %get-tuple-element.5) | data formatting | bytes 524288
Async XLA Ops:
  0.6 0.7 %copy-start = (s32[16,16]{1,0:T(8,128)S(1)}, s32[16,16]{1,0:T(8,128)}, u32[]{:S(2)}) copy-start(s32[16,16]{1,0:T(8,128)} %h_in.1) | copy-start | bytes 3076
where the time goes:
time: 34.3 us; the launch traced here: 34.1 us
  Pallas kernels  31.4 us (92%)
  local copies, waits for them, and re-layouts  2.1 us (6%)
  between operations  0.65 us (2%)
    pallas_call x1, Pallas kernels, per_device(): pl.pallas_call(functools.partial(kernel, nbx, nby), out_shape=(out, out),...  31.4 us
    unnamed x4, local copies, waits for them, and re-layouts  2.1 us

commit v1 on v0

v1 whole, which is shorter than its diff:
```python
import functools

import jax
import jax.numpy as jnp
from jax import lax
from jax.experimental import pallas as pl
from jax.experimental.pallas import tpu as pltpu
from jax.sharding import PartitionSpec as P_

DT_HJB = 0.5
NU_HJB = 0.25
COUPLE = 0.5
PENALTY = 2.0
DT_FP = 0.25
ABSORB = 4.0
SHIFT = 7.0

X0 = 4
HALO = 8
VMEM_LIMIT = 56_000_000
MESH = pl.DeviceIdType.MESH


class Link:
    def __init__(self, src, dst, send, recv, device, side):
        self.copy = pltpu.make_async_remote_copy(
            src_ref=src, dst_ref=dst, send_sem=send, recv_sem=recv,
            device_id=device, device_id_type=MESH)
        self.side = side


def kernel(nbx, nby, t_in, m_in, p_in, h_in, v_out, s_out,
           T, P, D, C, M, V, G, B1, Q, D4, HB, PA, PB,
           ssem, rsem, asend, arecv, bsend, brecv, lsem):
    nx, ny, nz = v_out.shape
    bx, by = lax.axis_index("bx"), lax.axis_index("by")
    XE, YE, X1 = nx + 2 * X0, ny + HALO, X0 + nx
    has = {-1: bx > 0, 1: bx < nbx - 1}
    hasy = {-1: by > 0, 1: by < nby - 1}

    def exists(dx, dy):
        if dx == 0:
            return hasy[dy]
        if dy == 0:
            return has[dx]
        return has[dx] & hasy[dy]

    sides = [(dx, dy) for dx in (-1, 0, 1) for dy in (-1, 0, 1) if (dx, dy) != (0, 0)]
    diagonals = [d for d in sides if d[0] and d[1]]
    there = {d: exists(*d) for d in sides}

    barrier = pltpu.get_barrier_semaphore()
    for k in range(1, nby):
        pl.semaphore_signal(barrier, inc=1, device_id=(bx, lax.rem(by + k, nby)), device_id_type=MESH)
    for k in range(1, nbx):
        pl.semaphore_signal(barrier, inc=1, device_id=(lax.rem(bx + k, nbx), by), device_id_type=MESH)
    greeted = (nby - 1) + (nbx - 1)
    for d in diagonals:
        @pl.when(there[d])
        def _():
            pl.semaphore_signal(barrier, inc=1, device_id=(bx + d[0], by + d[1]), device_id_type=MESH)
        greeted = greeted + there[d].astype(jnp.int32)

    rows = pl.ds(0, ny)
    beyond = pl.ds(ny, HALO)
    own = pl.ds(X0, nx)
    loads = [
        pltpu.make_async_copy(h_in, HB.at[1, 1], lsem.at[3]),
        pltpu.make_async_copy(m_in, D.at[own, rows], lsem.at[1]),
        pltpu.make_async_copy(p_in, P.at[own, rows], lsem.at[2]),
        pltpu.make_async_copy(t_in, T.at[own, rows], lsem.at[0]),
    ]
    for c in loads:
        c.start()

    count = [0]

    def link(src, dst, side):
        i = count[0]
        count[0] += 1
        return Link(src, dst, ssem.at[i], rsem.at[i], (bx + side[0], by + side[1]), side)

    def by_side(links):
        groups = {}
        for c in links:
            groups.setdefault(c.side, []).append(c)
        return groups

    def start(links):
        for side, group in by_side(links).items():
            @pl.when(there[side])
            def _():
                for c in group:
                    c.copy.start()

    def wait_recv(links):
        for side, group in by_side(links).items():
            @pl.when(there[(-side[0], -side[1])])
            def _():
                for c in group:
                    c.copy.wait_recv()

    def wait_send(links):
        for side, group in by_side(links).items():
            @pl.when(there[side])
            def _():
                for c in group:
                    c.copy.wait_send()

    def x_from(d, w):
        return pl.ds(nx - w, w) if d > 0 else pl.ds(0, w)

    def x_to(d, w):
        return pl.ds(X0 - w, w) if d > 0 else pl.ds(X1, w)

    def y_from(d, w):
        return pl.ds(ny - w, w) if d > 0 else pl.ds(0, w)

    def y_to(d, w):
        return pl.ds(YE - w, w) if d > 0 else pl.ds(ny, w)

    def input_link(src, dst, side, wx, wy):
        dx, dy = side
        xs = (x_from(dx, wx), x_to(dx, wx)) if dx else (pl.ds(0, nx), own)
        ys = (y_from(dy, wy), y_to(dy, wy)) if dy else (rows, rows)
        return link(src.at[xs[0], ys[0]], dst.at[xs[1], ys[1]], side)

    def field_link(side, wx, wy):
        dx, dy = side
        xs = (pl.ds(X1 - wx, wx), x_to(dx, wx)) if dx > 0 else (pl.ds(X0, wx), x_to(dx, wx))
        ys = (y_from(dy, wy), y_to(dy, wy)) if dy else (rows, rows)
        return link(G.at[xs[0], ys[0]], G.at[xs[1], ys[1]], side)

    def strips(planes):
        return [link(G.at[planes, y_from(d, w)], G.at[planes, y_to(d, w)], (0, d)) for d, w in ((1, 3), (-1, 4))]

    def heights_link(side):
        return link(h_in, HB.at[1 - side[0], 1 - side[1]], side)

    flat = [(-1, 0), (1, 0)]
    tall = [(0, -1), (0, 1)]
    hy = [heights_link(d) for d in tall]
    hx = [heights_link(d) for d in flat + diagonals]
    ty = [input_link(a, b, d, 0, w) for a, b, w in ((t_in, T, 3), (p_in, P, 2), (m_in, D, 2)) for d in tall]
    tx = [input_link(a, b, d, w, 0) for a, b, w in ((t_in, T, 3), (p_in, P, 2), (m_in, D, 2)) for d in flat]
    tc = [input_link(a, b, d, w, w) for a, b, w in ((t_in, T, 2), (p_in, P, 1), (m_in, D, 1)) for d in diagonals]

    def zero_planes(lo):
        for buf in (T, D, G):
            buf[pl.ds(lo, X0)] = jnp.zeros((X0, YE, nz), jnp.float32)

    def zero_rows(lo):
        for buf in (T, D, G):
            buf[:, pl.ds(lo, 4), :] = jnp.zeros((XE, 4, nz), jnp.float32)

    pl.when(jnp.logical_not(has[-1]))(lambda: zero_planes(0))
    pl.when(jnp.logical_not(has[1]))(lambda: zero_planes(X1))
    pl.when(jnp.logical_not(hasy[1]))(lambda: zero_rows(ny))
    pl.when(jnp.logical_not(hasy[-1]))(lambda: zero_rows(ny + 4))

    pl.semaphore_wait(barrier, greeted)
    start(hx + hy + ty + tx + tc)

    def column(side, part, x, n, first):
        line = HB[side, part, pl.ds(x, 1), :].astype(jnp.float32)
        lanes = lax.broadcasted_iota(jnp.int32, (n, ny), 1)
        subs = lax.broadcasted_iota(jnp.int32, (n, ny), 0) + first
        return jnp.sum(jnp.where(lanes == subs, line, 0.0), axis=1, keepdims=True)

    def level_mask(col, high):
        level = lax.broadcasted_iota(jnp.int32, (col.shape[0], nz), 1).astype(jnp.float32)
        return jnp.where(level < col, high, 0.0)

    def obstacles(side, x, i):
        D4[i, rows, :] = level_mask(column(side, 1, x, ny, 0), ABSORB)

    def beyond_obstacles(side, x, i):
        col = jnp.where(lax.broadcasted_iota(jnp.int32, (8, 1), 0) < 4,
                        column(side, 2, x, 8, 0), column(side, 0, x, 8, ny - 8))
        D4[i, beyond, :] = level_mask(col, ABSORB)

    def cost(i, part):
        C[i, part, :] = P[i, part, :] + COUPLE * D[i, part, :] + (PENALTY / ABSORB) * D4[i, part, :]

    row8 = lax.broadcasted_iota(jnp.int32, (8, nz), 0)
    keep = (row8 >= jnp.where(hasy[1], 0, 4)) & (row8 < jnp.where(hasy[-1], 8, 4))

    def loop(lo, hi, f):
        step = 4 if (hi - lo) % 4 == 0 else 1

        @pl.loop(0, (hi - lo) // step)
        def _(j):
            for k in range(step):
                f(lo + step * j + k)

    def pairs(lo, hi, value, store):
        @pl.loop(0, (hi - lo) // 2)
        def _(j):
            i = lo + 2 * j
            a, b = value(i), value(i + 1)
            store(i, a)
            store(i + 1, b)

    def each(planes, value, store):
        for i in planes:
            store(i, value(i))

    def ends(k, e, value, store):
        @pl.loop(0, k + e)
        def _(j):
            i, n = X0 - k + j, X1 - e + j
            a, b = value(i), value(n)
            store(i, a)
            store(n, b)

    def clear(buf, low, high):
        def zero(lo, k):
            buf[pl.ds(lo, k)] = jnp.zeros((k, YE, nz), jnp.float32)
        if low:
            pl.when(jnp.logical_not(has[-1]))(lambda: zero(X0 - low, low))
        if high:
            pl.when(jnp.logical_not(has[1]))(lambda: zero(X1, high))

    lane = lax.broadcasted_iota(jnp.int32, (YE, 128), 1)

    def z_up(v):
        n = v.shape[0]
        tiles = [pltpu.roll(v[:, j:j + 128], 127, 1) for j in range(0, nz, 128)]
        tiles.append(jnp.zeros_like(tiles[0]))
        return jnp.concatenate([jnp.where(lane[:n] == 127, b, a) for a, b in zip(tiles, tiles[1:])], axis=1)

    def z_low(v, edge=None):
        n = v.shape[0]
        tiles = [jnp.zeros((n, 128), jnp.float32) if edge is None else edge]
        tiles += [pltpu.roll(v[:, j:j + 128], 1, 1) for j in range(0, nz, 128)]
        return jnp.concatenate([jnp.where(lane[:n] == 0, a, b) for a, b in zip(tiles, tiles[1:])], axis=1)

    def put(dst, i, v):
        dst[i, rows, :] = v[:ny]
        dst[i, beyond, :] = jnp.where(keep, v[ny:], 0.0)

    def hjb(src):
        def f(i):
            v = src[i]
            lap = -6.0 * v
            ham = jnp.zeros_like(v)
            for u, l in ((src[i + 1], src[i - 1]), (pltpu.roll(v, YE - 1, 0), pltpu.roll(v, 1, 0)),
                         (z_up(v), z_low(v))):
                lap = lap + (u + l)
                ham = ham + jnp.square(jnp.maximum(v - l, 0.0)) + jnp.square(jnp.minimum(u - v, 0.0))
            return v + DT_HJB * (NU_HJB * lap - 0.5 * ham + C[i])
        return f

    def put_mid(i, v):
        put(M, i, v)

    def put_halo(i, v):
        put(V, i, v)

    def put_value(i, v):
        put(V, i, v)
        v_out[i - X0] = v[:ny]

    def flux(v, vu, m, mu):
        s = v - vu
        return jnp.maximum(s, 0.0) * m + jnp.minimum(s, 0.0) * mu

    def x_flux(i):
        return flux(V[i, rows, :], V[i + 1, rows, :], D[i, rows, :], D[i + 1, rows, :])

    def transport(starts, n):
        def one(i, before):
            v, m = V[i], D[i]
            fy = flux(v, pltpu.roll(v, YE - 1, 0), m, pltpu.roll(m, YE - 1, 0))
            ly = pltpu.roll(fy, 1, 0)[:ny]
            v, m = v[:ny], m[:ny]
            fz = flux(v, z_up(v), m, z_up(m))
            lz = z_low(fz, jnp.minimum(-v[:, :128], 0.0) * m[:, :128])
            fx = x_flux(i)
            return fx, m - DT_FP * ((fx - before) + (fy[:ny] - ly) + (fz - lz))

        def f(j, before):
            done = [one(lo + j, b) for lo, b in zip(starts, before)]
            for lo, d in zip(starts, done):
                G[lo + j, rows, :] = d[1]
            return tuple(d[0] for d in done)
        lax.fori_loop(0, n, f, tuple(x_flux(lo - 1) for lo in starts))

    half = nx // 2
    for c in loads[:3]:
        c.wait()

    def own_cost(i):
        obstacles(1, i - X0, i)
        cost(i, rows)

    loop(X0, X1, own_cost)
    wait_recv(hy + ty)

    def beyond_cost(i):
        beyond_obstacles(1, i - X0, i)
        cost(i, beyond)

    loop(X0, X1, beyond_cost)
    loads[3].wait()
    pairs(X0 + 1, X1 - 1, hjb(T), put_mid)
    pairs(X0 + 2, X1 - 2, hjb(M), put_value)
    transport((X0 + 3, X0 + half), half - 3)
    gi = strips(pl.ds(X0 + 3, nx - 6)) + [link(G.at[X0 + 3, rows], G.at[X1 + 3, rows], (-1, 0))]
    start(gi)

    wait_recv(hx)

    def halo_obstacles(side, x, i):
        obstacles(side, x, i)
        beyond_obstacles(side, x, i)

    for j in range(2):
        halo_obstacles(0, nx - 2 + j, X0 - 2 + j)
    for j in range(3):
        halo_obstacles(2, j, X1 + j)

    wait_recv(tx + tc)
    for i in (X0 - 2, X0 - 1, X1, X1 + 1):
        cost(i, pl.ds(0, YE))
    ends(2, 1, hjb(T), put_mid)
    clear(M, 2, 2)
    ends(0, 2, hjb(M), put_value)
    for i in (X0 - 1, X1):
        put_halo(i, hjb(M)(i))
    clear(V, 1, 1)
    transport((X0, X1 - 3), 3)

    gx = [field_link(d, 3, 0) for d in flat] + [field_link(d, 3, 3) for d in diagonals]
    gy = strips(pl.ds(X0, 3)) + strips(pl.ds(X1 - 3, 3))
    start(gx + gy)

    def shifted(src):
        def f(i):
            v = src[i]
            return D4[i] * v - ((src[i + 1] + src[i - 1]) + (pltpu.roll(v, YE - 1, 0) + pltpu.roll(v, 1, 0))
                                + (z_up(v) + z_low(v)))
        return f

    R = M

    def residual(i):
        return (1.0 - SHIFT) * G[i] - shifted(G)(i)

    def into(dst):
        return lambda i, v: put(dst, i, v)

    def moments(i, sums):
        r, b = R[i, rows, :], B1[i, rows, :]
        full = Q[i]
        yu = pltpu.roll(full, YE - 1, 0)[:ny]
        q = full[:ny]
        image = D4[i, rows, :] * q - 2.0 * (Q[i + 1, rows, :] + yu + z_up(q))
        terms = (r * r, r * b, b * b, b * q, q * q, q * image)

        def fold(a):
            a = a.reshape(ny // 8, 8, nz).sum(axis=0)
            return sum(a[:, j:j + 128] for j in range(0, nz, 128))

        return tuple(s + fold(a) for s, a in zip(sums, terms))

    wait_recv(gi[:2])
    pairs(X0 + 4, X1 - 4, residual, into(R))
    wait_recv(gy)
    ends(-1, 4, residual, into(R))
    pairs(X0 + 2, X1 - 2, shifted(R), into(B1))
    pairs(X0 + 3, X1 - 3, shifted(B1), into(Q))

    def two(j, sums):
        return moments(X0 + 4 + 2 * j, moments(X0 + 3 + 2 * j, sums))

    zero = jnp.zeros((8, 128), jnp.float32)
    sums = lax.fori_loop(0, (nx - 8) // 2, two, (zero,) * 6)

    wait_recv(gx + gi[2:])
    ends(2, 1, residual, into(R))
    into(R)(X1 + 2, residual(X1 + 2))
    clear(R, 2, 3)
    ends(1, 2, shifted(R), into(B1))
    into(B1)(X1 + 1, shifted(R)(X1 + 1))
    clear(B1, 1, 2)
    ends(0, 3, shifted(B1), into(Q))
    into(Q)(X1, shifted(B1)(X1))
    clear(Q, 0, 1)

    def rest(j, sums):
        for k in (2 * j, 2 * j + 1):
            sums = moments(X0 + k + jnp.where(k >= 3, nx - 8, 0), sums)
        return sums

    sums = lax.fori_loop(0, 4, rest, sums)
    tile_row = lax.broadcasted_iota(jnp.int32, (8, 128), 0)
    tile = zero
    for k, s in enumerate(sums):
        tile = jnp.where(tile_row == k, jnp.sum(s, axis=0, keepdims=True), tile)
    tile = jnp.sum(tile, axis=1, keepdims=True)
    tile = jnp.sum(jnp.where(tile_row == lane[:8], tile, 0.0), axis=0, keepdims=True)

    def all_sum(slots, value, n, me, device, send, recv):
        slots[me] = value
        copies = []
        for k in range(1, n):
            c = pltpu.make_async_remote_copy(
                src_ref=slots.at[me], dst_ref=slots.at[me], send_sem=send.at[k - 1], recv_sem=recv.at[k - 1],
                device_id=device(lax.rem(me + k, n)), device_id_type=MESH)
            c.start()
            copies.append(c)
        for k in range(1, n):
            source = lax.rem(me + n - k, n)
            pltpu.make_async_remote_copy(
                src_ref=slots.at[source], dst_ref=slots.at[source], send_sem=send.at[k - 1], recv_sem=recv.at[k - 1],
                device_id=device(source), device_id_type=MESH).wait_recv()
        return copies, jnp.sum(slots[...], axis=0)

    ca, tile = all_sum(PA, tile, nby, by, lambda j: (bx, j), asend, arecv)
    cb, tile = all_sum(PB, tile, nbx, bx, lambda j: (j, by), bsend, brecv)
    nu = [jnp.broadcast_to(tile[:, k:k + 1], (1, 128)) for k in range(6)]

    def dot(p, q, s):
        total = 0.0
        for i, a in enumerate(p):
            for j, b in enumerate(q):
                total = total + a * b * nu[i + j + s]
        return total

    def energy(p):
        return SHIFT * dot(p, p, 0) + dot(p, p, 1)

    def step_of(rr, p):
        return jnp.clip(rr / energy(p), 1.0 / 17.0, 1.0)

    one = jnp.ones_like(nu[0])
    rr = nu[0]
    p, r = (one,), (one,)
    x = None
    for it in range(3):
        a = step_of(rr, p)
        x = [a * c for c in p] if x is None else [x[j] + a * p[j] if j < len(x) else a * p[j] for j in range(len(p))]
        if it == 2:
            break
        image = [SHIFT * c for c in p] + [jnp.zeros_like(one)]
        for j, c in enumerate(p):
            image[j + 1] = image[j + 1] + c
        r = tuple((r[j] if j < len(r) else 0.0) - a * image[j] for j in range(len(image)))
        new = jnp.maximum(dot(r, r, 0), 0.0)
        beta = new / rr
        p = tuple(r[j] + (beta * p[j] if j < len(p) else 0.0) for j in range(len(r)))
        rr = new
    x = [jnp.concatenate([c] * (nz // 128), axis=1) for c in x]

    def finish(i):
        s_out[i - X0] = G[i, rows, :] + x[0] * R[i, rows, :] + x[1] * B1[i, rows, :] + x[2] * Q[i, rows, :]

    loop(X0, X1, finish)

    wait_send(hx + hy + ty + tx + tc + gi + gx + gy)
    for c in ca + cb:
        c.wait_send()


LINKS = 56


def write(v, s, v_out, s_out, sem):
    copies = [pltpu.make_async_copy(v, v_out, sem.at[0]), pltpu.make_async_copy(s, s_out, sem.at[1])]
    for c in copies:
        c.start()
    for c in copies:
        c.wait()


def per_device(nbx, nby, t, m, p, h):
    nx, ny, nz = t.shape
    ext = pltpu.VMEM((nx + 2 * X0, ny + HALO, nz), jnp.float32)
    out = jax.ShapeDtypeStruct(t.shape, jnp.float32)
    v, s = pl.pallas_call(
        functools.partial(kernel, nbx, nby),
        out_shape=(out, out),
        in_specs=[pl.BlockSpec(memory_space=pl.ANY)] * 4,
        out_specs=(pl.BlockSpec(memory_space=pltpu.VMEM),) * 2,
        scratch_shapes=[ext] * 10 + [
            pltpu.VMEM((3, 3, nx, ny), jnp.int32),
            pltpu.VMEM((nby, 1, 128), jnp.float32), pltpu.VMEM((nbx, 1, 128), jnp.float32),
            pltpu.SemaphoreType.DMA((LINKS,)), pltpu.SemaphoreType.DMA((LINKS,)),
            pltpu.SemaphoreType.DMA((nby - 1,)), pltpu.SemaphoreType.DMA((nby - 1,)),
            pltpu.SemaphoreType.DMA((nbx - 1,)), pltpu.SemaphoreType.DMA((nbx - 1,)),
            pltpu.SemaphoreType.DMA((4,)),
        ],
        compiler_params=pltpu.CompilerParams(collective_id=0, has_side_effects=True, vmem_limit_bytes=VMEM_LIMIT),
        name="mean_field_step",
    )(*(pltpu.with_memory_space_constraint(a, pltpu.HBM) for a in (t, m, p, h)))
    return pl.pallas_call(
        write,
        out_shape=(out, out),
        in_specs=[pl.BlockSpec(memory_space=pltpu.VMEM)] * 2,
        out_specs=(pl.BlockSpec(memory_space=pl.ANY),) * 2,
        scratch_shapes=[pltpu.SemaphoreType.DMA((2,))],
        compiler_params=pltpu.CompilerParams(vmem_limit_bytes=4_000_000),
        name="write",
    )(v, s)


def solution(mesh):
    cells, plane = P_("bx", "by", None), P_("bx", "by")
    return jax.shard_map(
        functools.partial(per_device, mesh.shape["bx"], mesh.shape["by"]),
        mesh=mesh, in_specs=(cells, cells, cells, plane), out_specs=(cells, cells), check_vma=False)
```

time: 34.3 us -> 30.9 us (0.901)
  local copies, waits for them, and re-layouts: 2.1 us -> 0 us
  Pallas kernels: 31.4 us -> 30.1 us
    pallas_call x1, Pallas kernels: 31.4 us -> 29.3 us  [per_device(): pl.pallas_call(functools.partial(kernel, nbx, nby), out_shape=(out, out),...]
    unnamed x4 -> x0, local copies, waits for them, and re-layouts: 2.1 us -> none
    pallas_call x0 -> x1, Pallas kernels: none -> 0.81 us  [per_device(): pl.pallas_call(write, out_shape=(out, out), in_specs=[pl.BlockSpec(memory...]
where the time goes in v1:
time: 30.9 us; the launch traced here: 30.7 us
  Pallas kernels  30.1 us (97%)
  between operations  0.64 us (2%)
    pallas_call x1, Pallas kernels, per_device(): pl.pallas_call(functools.partial(kernel, nbx, nby), out_shape=(out, out),...  29.3 us
    pallas_call x1, Pallas kernels, per_device(): pl.pallas_call(write, out_shape=(out, out), in_specs=[pl.BlockSpec(memory...  0.81 us

profile of v1, /device:TPU:0, one launch (start us, length us, event | category | flops | bytes accessed | tf_op | source)
XLA Modules:
  0.0 30.7 jit_solution(6436662900882534440)
XLA Ops:
  0.6 29.3 %mean_field_step.1 = (f32[16,16,256]{2,1,0:T(8,128)S(1)}, f32[16,16,256]{2,1,0:T(8,128)S(1)}) custom-call(f32[16,16,256]{2,1,0:T(8,128)} %t_in.1, f32[16,16,256]{2,1,0:T(8,128)} %m_in.1, f32[16,16,256]{2,1,0:T(8,128)} %p_in.1, s32[16,16]{1,0:T(8,128)} %h_in.1), custom_call_target="tpu_custom_call" | custom-call | tf_op jit(solution)/shard_map/mean_field_step/pallas_call | solution.py:481
  29.9 0.8 %write.1 = (f32[16,16,256]{2,1,0:T(8,128)}, f32[16,16,256]{2,1,0:T(8,128)}) custom-call(f32[16,16,256]{2,1,0:T(8,128)S(1)} %get-tuple-element.4.v, f32[16,16,256]{2,1,0:T(8,128)S(1)} %get-tuple-element.5.s), custom_call_target="tpu_custom_call" | custom-call | tf_op jit(solution)/shard_map/write/pallas_call | solution.py:497

commit v2 on v1

--- a/solution.py
+++ b/solution.py
@@ -17,20 +17,22 @@
 
 X0 = 4
 HALO = 8
+ONE_STAGE = 64
 VMEM_LIMIT = 56_000_000
 MESH = pl.DeviceIdType.MESH
 
 
 class Link:
-    def __init__(self, src, dst, send, recv, device, side):
+    def __init__(self, src, dst, send, recv, device, side, relay=None):
         self.copy = pltpu.make_async_remote_copy(
             src_ref=src, dst_ref=dst, send_sem=send, recv_sem=recv,
             device_id=device, device_id_type=MESH)
         self.side = side
+        self.relay = relay
 
 
 def kernel(nbx, nby, t_in, m_in, p_in, h_in, v_out, s_out,
-           T, P, D, C, M, V, G, B1, Q, D4, HB, PA, PB,
+           T, C, D, M, V, G, B1, Q, D4, POT, RB, HB, PA, PB,
            ssem, rsem, asend, arecv, bsend, brecv, lsem):
     nx, ny, nz = v_out.shape
     bx, by = lax.axis_index("bx"), lax.axis_index("by")
@@ -50,16 +52,22 @@
     there = {d: exists(*d) for d in sides}
 
     barrier = pltpu.get_barrier_semaphore()
-    for k in range(1, nby):
-        pl.semaphore_signal(barrier, inc=1, device_id=(bx, lax.rem(by + k, nby)), device_id_type=MESH)
-    for k in range(1, nbx):
-        pl.semaphore_signal(barrier, inc=1, device_id=(lax.rem(bx + k, nbx), by), device_id_type=MESH)
-    greeted = (nby - 1) + (nbx - 1)
-    for d in diagonals:
-        @pl.when(there[d])
-        def _():
-            pl.semaphore_signal(barrier, inc=1, device_id=(bx + d[0], by + d[1]), device_id_type=MESH)
-        greeted = greeted + there[d].astype(jnp.int32)
+    whole = nbx * nby <= ONE_STAGE
+    lines = [(0, j) for j in range(1, nby)] + [(i, 0) for i in range(1, nbx)]
+    peers = [(i, j) for j in range(nby) for i in range(nbx) if (i, j) != (0, 0)] if whole else lines
+
+    def peer(i, j):
+        return lax.rem(bx + i, nbx), lax.rem(by + j, nby)
+
+    for d in peers:
+        pl.semaphore_signal(barrier, inc=1, device_id=peer(*d), device_id_type=MESH)
+    greeted = len(peers)
+    if not whole:
+        for d in diagonals:
+            @pl.when(there[d])
+            def _():
+                pl.semaphore_signal(barrier, inc=1, device_id=(bx + d[0], by + d[1]), device_id_type=MESH)
+            greeted = greeted + there[d].astype(jnp.int32)
 
     rows = pl.ds(0, ny)
     beyond = pl.ds(ny, HALO)
@@ -67,7 +75,7 @@
     loads = [
         pltpu.make_async_copy(h_in, HB.at[1, 1], lsem.at[3]),
         pltpu.make_async_copy(m_in, D.at[own, rows], lsem.at[1]),
-        pltpu.make_async_copy(p_in, P.at[own, rows], lsem.at[2]),
+        pltpu.make_async_copy(p_in, POT, lsem.at[2]),
         pltpu.make_async_copy(t_in, T.at[own, rows], lsem.at[0]),
     ]
     for c in loads:
@@ -75,34 +83,39 @@
 
     count = [0]
 
-    def link(src, dst, side):
+    def link(src, dst, side, relay=None):
         i = count[0]
         count[0] += 1
-        return Link(src, dst, ssem.at[i], rsem.at[i], (bx + side[0], by + side[1]), side)
-
-    def by_side(links):
+        return Link(src, dst, ssem.at[i], rsem.at[i], (bx + side[0], by + side[1]), side, relay)
+
+    def grouped(links, sends):
         groups = {}
         for c in links:
-            groups.setdefault(c.side, []).append(c)
-        return groups
+            groups.setdefault((c.side, c.relay), []).append(c)
+        for (side, relay), group in groups.items():
+            if relay is not None:
+                here = bx == relay[0 if sends else 1]
+            else:
+                here = there[side] if sends else there[(-side[0], -side[1])]
+            yield here, group
 
     def start(links):
-        for side, group in by_side(links).items():
-            @pl.when(there[side])
+        for here, group in grouped(links, True):
+            @pl.when(here)
             def _():
                 for c in group:
                     c.copy.start()
 
     def wait_recv(links):
-        for side, group in by_side(links).items():
-            @pl.when(there[(-side[0], -side[1])])
+        for here, group in grouped(links, False):
+            @pl.when(here)
             def _():
                 for c in group:
                     c.copy.wait_recv()
 
     def wait_send(links):
-        for side, group in by_side(links).items():
-            @pl.when(there[side])
+        for here, group in grouped(links, True):
+            @pl.when(here)
             def _():
                 for c in group:
                     c.copy.wait_send()
@@ -125,11 +138,11 @@
         ys = (y_from(dy, wy), y_to(dy, wy)) if dy else (rows, rows)
         return link(src.at[xs[0], ys[0]], dst.at[xs[1], ys[1]], side)
 
-    def field_link(side, wx, wy):
+    def field_link(buf, side, wx, wy):
         dx, dy = side
-        xs = (pl.ds(X1 - wx, wx), x_to(dx, wx)) if dx > 0 else (pl.ds(X0, wx), x_to(dx, wx))
+        xs = (pl.ds(X1 - wx, wx) if dx > 0 else pl.ds(X0, wx), x_to(dx, wx)) if dx else (own, own)
         ys = (y_from(dy, wy), y_to(dy, wy)) if dy else (rows, rows)
-        return link(G.at[xs[0], ys[0]], G.at[xs[1], ys[1]], side)
+        return link(buf.at[xs[0], ys[0]], buf.at[xs[1], ys[1]], side)
 
     def strips(planes):
         return [link(G.at[planes, y_from(d, w)], G.at[planes, y_to(d, w)], (0, d)) for d, w in ((1, 3), (-1, 4))]
@@ -141,9 +154,19 @@
     tall = [(0, -1), (0, 1)]
     hy = [heights_link(d) for d in tall]
     hx = [heights_link(d) for d in flat + diagonals]
-    ty = [input_link(a, b, d, 0, w) for a, b, w in ((t_in, T, 3), (p_in, P, 2), (m_in, D, 2)) for d in tall]
-    tx = [input_link(a, b, d, w, 0) for a, b, w in ((t_in, T, 3), (p_in, P, 2), (m_in, D, 2)) for d in flat]
-    tc = [input_link(a, b, d, w, w) for a, b, w in ((t_in, T, 2), (p_in, P, 1), (m_in, D, 1)) for d in diagonals]
+    ty = [input_link(t_in, T, d, 0, 3) for d in tall] + [field_link(C, d, 0, 2) for d in tall]
+    dy = [input_link(m_in, D, d, 0, 1) for d in tall]
+    tx = [input_link(t_in, T, d, 2, 2) for d in diagonals]
+    first, second = [], []
+    if nbx == 4:
+        tops, lows = (t_in.at[x_from(1, 3)], T.at[x_to(1, 3), rows]), (t_in.at[x_from(-1, 3)], T.at[x_to(-1, 3), rows])
+        first = [link(tops[0], RB, (2, 0), (1, 3)), link(lows[0], RB, (-2, 0), (2, 0))]
+        tx += [link(*tops, (1, 0), (0, 1)), link(*tops, (1, 0), (2, 3)), link(*lows, (-1, 0), (1, 0)), link(*lows, (-1, 0), (3, 2))]
+        second = [link(RB, tops[1], (-1, 0), (3, 2)), link(RB, lows[1], (1, 0), (0, 1))]
+    else:
+        tx += [input_link(t_in, T, d, 3, 0) for d in flat]
+    cx = [field_link(C, d, 2, 0) for d in flat] + [field_link(C, d, 1, 1) for d in diagonals]
+    dx = [input_link(m_in, D, d, 1, 0) for d in flat]
 
     def zero_planes(lo):
         for buf in (T, D, G):
@@ -157,9 +180,6 @@
     pl.when(jnp.logical_not(has[1]))(lambda: zero_planes(X1))
     pl.when(jnp.logical_not(hasy[1]))(lambda: zero_rows(ny))
     pl.when(jnp.logical_not(hasy[-1]))(lambda: zero_rows(ny + 4))
-
-    pl.semaphore_wait(barrier, greeted)
-    start(hx + hy + ty + tx + tc)
 
     def column(side, part, x, n, first):
         line = HB[side, part, pl.ds(x, 1), :].astype(jnp.float32)
@@ -180,7 +200,7 @@
         D4[i, beyond, :] = level_mask(col, ABSORB)
 
     def cost(i, part):
-        C[i, part, :] = P[i, part, :] + COUPLE * D[i, part, :] + (PENALTY / ABSORB) * D4[i, part, :]
+        C[i, part, :] = POT[i - X0] + COUPLE * D[i, part, :] + (PENALTY / ABSORB) * D4[i, part, :]
 
     row8 = lax.broadcasted_iota(jnp.int32, (8, nz), 0)
     keep = (row8 >= jnp.where(hasy[1], 0, 4)) & (row8 < jnp.where(hasy[-1], 8, 4))
@@ -295,20 +315,21 @@
         cost(i, rows)
 
     loop(X0, X1, own_cost)
-    wait_recv(hy + ty)
-
-    def beyond_cost(i):
-        beyond_obstacles(1, i - X0, i)
-        cost(i, beyond)
-
-    loop(X0, X1, beyond_cost)
+    pl.semaphore_wait(barrier, greeted)
+    start(first + ty + dy + tx + cx + dx + hx + hy)
     loads[3].wait()
+    wait_recv(ty)
+    wait_recv(first)
+    start(second)
     pairs(X0 + 1, X1 - 1, hjb(T), put_mid)
     pairs(X0 + 2, X1 - 2, hjb(M), put_value)
+    wait_recv(dy)
     transport((X0 + 3, X0 + half), half - 3)
     gi = strips(pl.ds(X0 + 3, nx - 6)) + [link(G.at[X0 + 3, rows], G.at[X1 + 3, rows], (-1, 0))]
     start(gi)
 
+    wait_recv(hy)
+    loop(X0, X1, lambda i: beyond_obstacles(1, i - X0, i))
     wait_recv(hx)
 
     def halo_obstacles(side, x, i):
@@ -320,20 +341,19 @@
     for j in range(3):
         halo_obstacles(2, j, X1 + j)
 
-    wait_recv(tx + tc)
-    for i in (X0 - 2, X0 - 1, X1, X1 + 1):
-        cost(i, pl.ds(0, YE))
+    wait_recv(tx + cx + second)
     ends(2, 1, hjb(T), put_mid)
     clear(M, 2, 2)
     ends(0, 2, hjb(M), put_value)
     for i in (X0 - 1, X1):
         put_halo(i, hjb(M)(i))
     clear(V, 1, 1)
+    wait_recv(dx)
     transport((X0, X1 - 3), 3)
 
-    gx = [field_link(d, 3, 0) for d in flat] + [field_link(d, 3, 3) for d in diagonals]
+    gx = [field_link(G, d, 3, 0) for d in flat] + [field_link(G, d, 3, 3) for d in diagonals]
     gy = strips(pl.ds(X0, 3)) + strips(pl.ds(X1 - 3, 3))
-    start(gx + gy)
+    start(gy + gx)
 
     def shifted(src):
         def f(i):
@@ -417,8 +437,27 @@
                 device_id=device(source), device_id_type=MESH).wait_recv()
         return copies, jnp.sum(slots[...], axis=0)
 
-    ca, tile = all_sum(PA, tile, nby, by, lambda j: (bx, j), asend, arecv)
-    cb, tile = all_sum(PB, tile, nbx, bx, lambda j: (j, by), bsend, brecv)
+    if whole:
+        me = bx * nby + by
+        PA[me] = tile
+        ca, cb = [], []
+        order = sorted(range(len(peers)), key=lambda k: -min(peers[k][1], nby - peers[k][1]))
+        for k in order:
+            c = pltpu.make_async_remote_copy(
+                src_ref=PA.at[me], dst_ref=PA.at[me], send_sem=asend.at[k], recv_sem=arecv.at[k],
+                device_id=peer(*peers[k]), device_id_type=MESH)
+            c.start()
+            ca.append(c)
+        for k in order:
+            x, y = peer(nbx - peers[k][0], nby - peers[k][1])
+            source = x * nby + y
+            pltpu.make_async_remote_copy(
+                src_ref=PA.at[source], dst_ref=PA.at[source], send_sem=asend.at[k], recv_sem=arecv.at[k],
+                device_id=(x, y), device_id_type=MESH).wait_recv()
+        tile = jnp.sum(PA[...], axis=0)
+    else:
+        ca, tile = all_sum(PA, tile, nby, by, lambda j: (bx, j), asend, arecv)
+        cb, tile = all_sum(PB, tile, nbx, bx, lambda j: (j, by), bsend, brecv)
     nu = [jnp.broadcast_to(tile[:, k:k + 1], (1, 128)) for k in range(6)]
 
     def dot(p, q, s):
@@ -458,12 +497,12 @@
 
     loop(X0, X1, finish)
 
-    wait_send(hx + hy + ty + tx + tc + gi + gx + gy)
+    wait_send(first + second + hx + hy + ty + dy + tx + cx + dx + gi + gx + gy)
     for c in ca + cb:
         c.wait_send()
 
 
-LINKS = 56
+LINKS = 64
 
 
 def write(v, s, v_out, s_out, sem):
@@ -476,6 +515,7 @@
 
 def per_device(nbx, nby, t, m, p, h):
     nx, ny, nz = t.shape
+    slots = nbx * nby if nbx * nby <= ONE_STAGE else nby
     ext = pltpu.VMEM((nx + 2 * X0, ny + HALO, nz), jnp.float32)
     out = jax.ShapeDtypeStruct(t.shape, jnp.float32)
     v, s = pl.pallas_call(
@@ -483,11 +523,13 @@
         out_shape=(out, out),
         in_specs=[pl.BlockSpec(memory_space=pl.ANY)] * 4,
         out_specs=(pl.BlockSpec(memory_space=pltpu.VMEM),) * 2,
-        scratch_shapes=[ext] * 10 + [
+        scratch_shapes=[ext] * 9 + [
+            pltpu.VMEM((nx, ny, nz), jnp.float32),
+            pltpu.VMEM((3, ny, nz), jnp.float32),
             pltpu.VMEM((3, 3, nx, ny), jnp.int32),
-            pltpu.VMEM((nby, 1, 128), jnp.float32), pltpu.VMEM((nbx, 1, 128), jnp.float32),
+            pltpu.VMEM((slots, 1, 128), jnp.float32), pltpu.VMEM((nbx, 1, 128), jnp.float32),
             pltpu.SemaphoreType.DMA((LINKS,)), pltpu.SemaphoreType.DMA((LINKS,)),
-            pltpu.SemaphoreType.DMA((nby - 1,)), pltpu.SemaphoreType.DMA((nby - 1,)),
+            pltpu.SemaphoreType.DMA((slots - 1,)), pltpu.SemaphoreType.DMA((slots - 1,)),
             pltpu.SemaphoreType.DMA((nbx - 1,)), pltpu.SemaphoreType.DMA((nbx - 1,)),
             pltpu.SemaphoreType.DMA((4,)),
         ],

time: 30.9 us -> 27.9 us (0.903)
  Pallas kernels: 30.1 us -> 27.1 us
    pallas_call x1, Pallas kernels: 29.3 us -> 26.3 us  [per_device(): pl.pallas_call(functools.partial(kernel, nbx, nby), out_shape=(out, out),...]
where the time goes in v2:
time: 27.9 us; the launch traced here: 27.7 us
  Pallas kernels  27.1 us (97%)
  between operations  0.64 us (2%)
    pallas_call x1, Pallas kernels, per_device(): pl.pallas_call(functools.partial(kernel, nbx, nby), out_shape=(out, out),...  26.3 us
    pallas_call x1, Pallas kernels, per_device(): pl.pallas_call(write, out_shape=(out, out), in_specs=[pl.BlockSpec(memory...  0.81 us

profile of v2, /device:TPU:0, one launch (start us, length us, event | category | flops | bytes accessed | tf_op | source)
XLA Modules:
  0.0 27.7 jit_solution(2200900225392933184)
XLA Ops:
  0.6 26.3 %mean_field_step.1 = (f32[16,16,256]{2,1,0:T(8,128)S(1)}, f32[16,16,256]{2,1,0:T(8,128)S(1)}) custom-call(f32[16,16,256]{2,1,0:T(8,128)} %t_in.1, f32[16,16,256]{2,1,0:T(8,128)} %m_in.1, f32[16,16,256]{2,1,0:T(8,128)} %p_in.1, s32[16,16]{1,0:T(8,128)} %h_in.1), custom_call_target="tpu_custom_call" | custom-call | tf_op jit(solution)/shard_map/mean_field_step/pallas_call | solution.py:521
  26.9 0.8 %write.1 = (f32[16,16,256]{2,1,0:T(8,128)}, f32[16,16,256]{2,1,0:T(8,128)}) custom-call(f32[16,16,256]{2,1,0:T(8,128)S(1)} %get-tuple-element.4.v, f32[16,16,256]{2,1,0:T(8,128)S(1)} %get-tuple-element.5.s), custom_call_target="tpu_custom_call" | custom-call | tf_op jit(solution)/shard_map/write/pallas_call | solution.py:539

commit v3 on v2

--- a/solution.py
+++ b/solution.py
@@ -17,7 +17,6 @@
 
 X0 = 4
 HALO = 8
-ONE_STAGE = 64
 VMEM_LIMIT = 56_000_000
 MESH = pl.DeviceIdType.MESH
 
@@ -33,7 +32,7 @@
 
 def kernel(nbx, nby, t_in, m_in, p_in, h_in, v_out, s_out,
            T, C, D, M, V, G, B1, Q, D4, POT, RB, HB, PA, PB,
-           ssem, rsem, asend, arecv, bsend, brecv, lsem):
+           ssem, rsem, asend, arecv, bsend, brecv, lsem, token):
     nx, ny, nz = v_out.shape
     bx, by = lax.axis_index("bx"), lax.axis_index("by")
     XE, YE, X1 = nx + 2 * X0, ny + HALO, X0 + nx
@@ -52,22 +51,41 @@
     there = {d: exists(*d) for d in sides}
 
     barrier = pltpu.get_barrier_semaphore()
-    whole = nbx * nby <= ONE_STAGE
+    whole = nbx <= 4 and nby <= 8
     lines = [(0, j) for j in range(1, nby)] + [(i, 0) for i in range(1, nbx)]
     peers = [(i, j) for j in range(nby) for i in range(nbx) if (i, j) != (0, 0)] if whole else lines
 
     def peer(i, j):
         return lax.rem(bx + i, nbx), lax.rem(by + j, nby)
 
-    for d in peers:
-        pl.semaphore_signal(barrier, inc=1, device_id=peer(*d), device_id_type=MESH)
-    greeted = len(peers)
-    if not whole:
-        for d in diagonals:
-            @pl.when(there[d])
+    greeted = 0
+    if whole:
+        greet = sides
+        if nbx == 4:
+            pl.semaphore_signal(barrier, inc=1, device_id=peer(2, 0), device_id_type=MESH)
+            greeted = 1
+    else:
+        greet = diagonals
+        for d in lines:
+            pl.semaphore_signal(barrier, inc=1, device_id=peer(*d), device_id_type=MESH)
+        greeted = len(lines)
+    for d in greet:
+        @pl.when(there[d])
+        def _():
+            pl.semaphore_signal(barrier, inc=1, device_id=(bx + d[0], by + d[1]), device_id_type=MESH)
+        greeted = greeted + there[d].astype(jnp.int32)
+
+    def far(k):
+        return (by >= k, by - k), (by < nby - k, by + k)
+
+    def tell(k, sem):
+        for here, j in far(k):
+            @pl.when(here)
             def _():
-                pl.semaphore_signal(barrier, inc=1, device_id=(bx + d[0], by + d[1]), device_id_type=MESH)
-            greeted = greeted + there[d].astype(jnp.int32)
+                pl.semaphore_signal(sem, inc=1, device_id=(bx, j), device_id_type=MESH)
+
+    def hear(k, sem):
+        pl.semaphore_wait(sem, sum(here.astype(jnp.int32) for here, _ in far(k)))
 
     rows = pl.ds(0, ny)
     beyond = pl.ds(ny, HALO)
@@ -154,7 +172,8 @@
     tall = [(0, -1), (0, 1)]
     hy = [heights_link(d) for d in tall]
     hx = [heights_link(d) for d in flat + diagonals]
-    ty = [input_link(t_in, T, d, 0, 3) for d in tall] + [field_link(C, d, 0, 2) for d in tall]
+    ty = [input_link(t_in, T, d, 0, 3) for d in tall]
+    cy = [field_link(C, d, 0, 2) for d in tall]
     dy = [input_link(m_in, D, d, 0, 1) for d in tall]
     tx = [input_link(t_in, T, d, 2, 2) for d in diagonals]
     first, second = [], []
@@ -307,6 +326,8 @@
         lax.fori_loop(0, n, f, tuple(x_flux(lo - 1) for lo in starts))
 
     half = nx // 2
+    pl.semaphore_wait(barrier, greeted)
+    start(first + ty + tx)
     for c in loads[:3]:
         c.wait()
 
@@ -315,10 +336,9 @@
         cost(i, rows)
 
     loop(X0, X1, own_cost)
-    pl.semaphore_wait(barrier, greeted)
-    start(first + ty + dy + tx + cx + dx + hx + hy)
+    start(cy + cx + dy + dx + hx + hy)
     loads[3].wait()
-    wait_recv(ty)
+    wait_recv(ty + cy)
     wait_recv(first)
     start(second)
     pairs(X0 + 1, X1 - 1, hjb(T), put_mid)
@@ -354,6 +374,8 @@
     gx = [field_link(G, d, 3, 0) for d in flat] + [field_link(G, d, 3, 3) for d in diagonals]
     gy = strips(pl.ds(X0, 3)) + strips(pl.ds(X1 - 3, 3))
     start(gy + gx)
+    if whole:
+        tell(2, token.at[0])
 
     def shifted(src):
         def f(i):
@@ -398,6 +420,9 @@
     sums = lax.fori_loop(0, (nx - 8) // 2, two, (zero,) * 6)
 
     wait_recv(gx + gi[2:])
+    if whole:
+        hear(2, token.at[0])
+        tell(4, token.at[1])
     ends(2, 1, residual, into(R))
     into(R)(X1 + 2, residual(X1 + 2))
     clear(R, 2, 3)
@@ -438,6 +463,7 @@
         return copies, jnp.sum(slots[...], axis=0)
 
     if whole:
+        hear(4, token.at[1])
         me = bx * nby + by
         PA[me] = tile
         ca, cb = [], []
@@ -497,7 +523,7 @@
 
     loop(X0, X1, finish)
 
-    wait_send(first + second + hx + hy + ty + dy + tx + cx + dx + gi + gx + gy)
+    wait_send(first + second + hx + hy + ty + cy + dy + tx + cx + dx + gi + gx + gy)
     for c in ca + cb:
         c.wait_send()
 
@@ -515,7 +541,7 @@
 
 def per_device(nbx, nby, t, m, p, h):
     nx, ny, nz = t.shape
-    slots = nbx * nby if nbx * nby <= ONE_STAGE else nby
+    slots = nbx * nby if nbx <= 4 and nby <= 8 else nby
     ext = pltpu.VMEM((nx + 2 * X0, ny + HALO, nz), jnp.float32)
     out = jax.ShapeDtypeStruct(t.shape, jnp.float32)
     v, s = pl.pallas_call(
@@ -531,7 +557,7 @@
             pltpu.SemaphoreType.DMA((LINKS,)), pltpu.SemaphoreType.DMA((LINKS,)),
             pltpu.SemaphoreType.DMA((slots - 1,)), pltpu.SemaphoreType.DMA((slots - 1,)),
             pltpu.SemaphoreType.DMA((nbx - 1,)), pltpu.SemaphoreType.DMA((nbx - 1,)),
-            pltpu.SemaphoreType.DMA((4,)),
+            pltpu.SemaphoreType.DMA((4,)), pltpu.SemaphoreType.REGULAR((2,)),
         ],
         compiler_params=pltpu.CompilerParams(collective_id=0, has_side_effects=True, vmem_limit_bytes=VMEM_LIMIT),
         name="mean_field_step",

time: 27.9 us -> 27.7 us (level)
  no operation moved by 1% of the time
where the time goes in v3:
time: 27.7 us; the launch traced here: 27.6 us
  Pallas kernels  26.9 us (97%)
  between operations  0.64 us (2%)
    pallas_call x1, Pallas kernels, per_device(): pl.pallas_call(functools.partial(kernel, nbx, nby), out_shape=(out, out),...  26.1 us
    pallas_call x1, Pallas kernels, per_device(): pl.pallas_call(write, out_shape=(out, out), in_specs=[pl.BlockSpec(memory...  0.81 us

profile of v3, /device:TPU:0, one launch (start us, length us, event | category | flops | bytes accessed | tf_op | source)
XLA Modules:
  0.0 27.6 jit_solution(16232972198421553169)
XLA Ops:
  0.6 26.1 %mean_field_step.1 = (f32[16,16,256]{2,1,0:T(8,128)S(1)}, f32[16,16,256]{2,1,0:T(8,128)S(1)}) custom-call(f32[16,16,256]{2,1,0:T(8,128)} %t_in.1, f32[16,16,256]{2,1,0:T(8,128)} %m_in.1, f32[16,16,256]{2,1,0:T(8,128)} %p_in.1, s32[16,16]{1,0:T(8,128)} %h_in.1), custom_call_target="tpu_custom_call" | custom-call | tf_op jit(solution)/shard_map/mean_field_step/pallas_call | solution.py:547
  26.8 0.8 %write.1 = (f32[16,16,256]{2,1,0:T(8,128)}, f32[16,16,256]{2,1,0:T(8,128)}) custom-call(f32[16,16,256]{2,1,0:T(8,128)S(1)} %get-tuple-element.4.v, f32[16,16,256]{2,1,0:T(8,128)S(1)} %get-tuple-element.5.s), custom_call_target="tpu_custom_call" | custom-call | tf_op jit(solution)/shard_map/write/pallas_call | solution.py:565

commit v4 on v3

--- a/solution.py
+++ b/solution.py
@@ -446,44 +446,27 @@
     tile = jnp.sum(tile, axis=1, keepdims=True)
     tile = jnp.sum(jnp.where(tile_row == lane[:8], tile, 0.0), axis=0, keepdims=True)
 
-    def all_sum(slots, value, n, me, device, send, recv):
+    def all_sum(slots, value, me, near, send, recv):
         slots[me] = value
-        copies = []
-        for k in range(1, n):
-            c = pltpu.make_async_remote_copy(
-                src_ref=slots.at[me], dst_ref=slots.at[me], send_sem=send.at[k - 1], recv_sem=recv.at[k - 1],
-                device_id=device(lax.rem(me + k, n)), device_id_type=MESH)
-            c.start()
-            copies.append(c)
-        for k in range(1, n):
-            source = lax.rem(me + n - k, n)
+        for d in near:
             pltpu.make_async_remote_copy(
-                src_ref=slots.at[source], dst_ref=slots.at[source], send_sem=send.at[k - 1], recv_sem=recv.at[k - 1],
-                device_id=device(source), device_id_type=MESH).wait_recv()
-        return copies, jnp.sum(slots[...], axis=0)
+                src_ref=slots.at[me], dst_ref=slots.at[me], send_sem=send.at[0], recv_sem=recv.at[0],
+                device_id=peer(*d), device_id_type=MESH).start()
+        area = slots.at[pl.ds(0, len(near))]
+        every = pltpu.make_async_remote_copy(
+            src_ref=area, dst_ref=area, send_sem=send.at[0], recv_sem=recv.at[0],
+            device_id=peer(*near[0]), device_id_type=MESH)
+        every.wait_recv()
+        return [every], jnp.sum(slots[...], axis=0)
 
     if whole:
         hear(4, token.at[1])
-        me = bx * nby + by
-        PA[me] = tile
-        ca, cb = [], []
-        order = sorted(range(len(peers)), key=lambda k: -min(peers[k][1], nby - peers[k][1]))
-        for k in order:
-            c = pltpu.make_async_remote_copy(
-                src_ref=PA.at[me], dst_ref=PA.at[me], send_sem=asend.at[k], recv_sem=arecv.at[k],
-                device_id=peer(*peers[k]), device_id_type=MESH)
-            c.start()
-            ca.append(c)
-        for k in order:
-            x, y = peer(nbx - peers[k][0], nby - peers[k][1])
-            source = x * nby + y
-            pltpu.make_async_remote_copy(
-                src_ref=PA.at[source], dst_ref=PA.at[source], send_sem=asend.at[k], recv_sem=arecv.at[k],
-                device_id=(x, y), device_id_type=MESH).wait_recv()
-        tile = jnp.sum(PA[...], axis=0)
+        order = sorted(peers, key=lambda d: -min(d[1], nby - d[1]))
+        ca, tile = all_sum(PA, tile, bx * nby + by, order, asend, arecv)
+        cb = []
     else:
-        ca, tile = all_sum(PA, tile, nby, by, lambda j: (bx, j), asend, arecv)
-        cb, tile = all_sum(PB, tile, nbx, bx, lambda j: (j, by), bsend, brecv)
+        ca, tile = all_sum(PA, tile, by, lines[:nby - 1], asend, arecv)
+        cb, tile = all_sum(PB, tile, bx, lines[nby - 1:], bsend, brecv)
     nu = [jnp.broadcast_to(tile[:, k:k + 1], (1, 128)) for k in range(6)]
 
     def dot(p, q, s):
@@ -528,7 +511,7 @@
         c.wait_send()
 
 
-LINKS = 64
+LINKS = 49
 
 
 def write(v, s, v_out, s_out, sem):
@@ -555,8 +538,8 @@
             pltpu.VMEM((3, 3, nx, ny), jnp.int32),
             pltpu.VMEM((slots, 1, 128), jnp.float32), pltpu.VMEM((nbx, 1, 128), jnp.float32),
             pltpu.SemaphoreType.DMA((LINKS,)), pltpu.SemaphoreType.DMA((LINKS,)),
-            pltpu.SemaphoreType.DMA((slots - 1,)), pltpu.SemaphoreType.DMA((slots - 1,)),
-            pltpu.SemaphoreType.DMA((nbx - 1,)), pltpu.SemaphoreType.DMA((nbx - 1,)),
+            pltpu.SemaphoreType.DMA((1,)), pltpu.SemaphoreType.DMA((1,)),
+            pltpu.SemaphoreType.DMA((1,)), pltpu.SemaphoreType.DMA((1,)),
             pltpu.SemaphoreType.DMA((4,)), pltpu.SemaphoreType.REGULAR((2,)),
         ],
         compiler_params=pltpu.CompilerParams(collective_id=0, has_side_effects=True, vmem_limit_bytes=VMEM_LIMIT),

time: 27.7 us -> 26.8 us (0.968)
  Pallas kernels: 26.9 us -> 26 us
    pallas_call x1, Pallas kernels: 26.1 us -> 25.2 us  [per_device(): pl.pallas_call(functools.partial(kernel, nbx, nby), out_shape=(out, out),...]
where the time goes in v4:
time: 26.8 us; the launch traced here: 26.7 us
  Pallas kernels  26 us (97%)
  between operations  0.64 us (2%)
    pallas_call x1, Pallas kernels, per_device(): pl.pallas_call(functools.partial(kernel, nbx, nby), out_shape=(out, out),...  25.2 us
    pallas_call x1, Pallas kernels, per_device(): pl.pallas_call(write, out_shape=(out, out), in_specs=[pl.BlockSpec(memory...  0.81 us

profile of v4, /device:TPU:0, one launch (start us, length us, event | category | flops | bytes accessed | tf_op | source)
XLA Modules:
  0.0 26.7 jit_solution(17193413405679564292)
XLA Ops:
  0.6 25.2 %mean_field_step.1 = (f32[16,16,256]{2,1,0:T(8,128)S(1)}, f32[16,16,256]{2,1,0:T(8,128)S(1)}) custom-call(f32[16,16,256]{2,1,0:T(8,128)} %t_in.1, f32[16,16,256]{2,1,0:T(8,128)} %m_in.1, f32[16,16,256]{2,1,0:T(8,128)} %p_in.1, s32[16,16]{1,0:T(8,128)} %h_in.1), custom_call_target="tpu_custom_call" | custom-call | tf_op jit(solution)/shard_map/mean_field_step/pallas_call | solution.py:530
  25.9 0.8 %write.1 = (f32[16,16,256]{2,1,0:T(8,128)}, f32[16,16,256]{2,1,0:T(8,128)}) custom-call(f32[16,16,256]{2,1,0:T(8,128)S(1)} %get-tuple-element.4.v, f32[16,16,256]{2,1,0:T(8,128)S(1)} %get-tuple-element.5.s), custom_call_target="tpu_custom_call" | custom-call | tf_op jit(solution)/shard_map/write/pallas_call | solution.py:548
